TPU v7x, 256 devices: a whole 4x4x8 slice. The times are simulated.
256 devices in a mesh: ctx: 32 (over x_lo, z, core), ep: 8 (over y, x_hi).
Axes of the slice: x: 4 (x_hi: 2, x_lo: 2; x = x_hi * 2 + x_lo), y: 4, z: 8, core: 2. Of those that a mesh axis runs over, the one named last changes fastest.
Arguments:
- queries: bfloat16 [4096, 6144], P('ctx', 'ep'), may hold values from -8 to 8
- keys: bfloat16 [4096, 1024], P('ctx', 'ep'), may hold values from -4 to 4
- values: bfloat16 [4096, 1024], P('ctx', 'ep'), may hold values from -13.5 to 13.5
- gate_weight: bfloat16 [32, 6144, 2048], P('ctx', 'ep'), may hold values from -0.078125 to 0.078125
- up_weight: bfloat16 [32, 6144, 2048], P('ctx', 'ep'), may hold values from -0.078125 to 0.078125
- down_weight: bfloat16 [32, 2048, 6144], P('ctx', None, 'ep'), may hold values from -0.125 to 0.125
- expert_ids: int32 [4096, 2], P('ctx'), may hold values from 0 to 31, as said below
- route_logits: float32 [4096, 2], P('ctx'), may hold values from -6 to 6
Outputs:
- layer_out: bfloat16 [4096, 6144], P('ctx', 'ep')
Inputs may be any that keep to these rules, and one draw needn't show every extreme that they name: `expert_ids`: the two experts of a position differ. In every sequence block of 128 positions the same 2 experts are named exactly 24 times each, one further expert is named exactly 12 times, and every other expert is named at least once and at most 12 times.
All inputs are finite; a program needn't handle non-finite values.
Results may differ from a plain program's by a relative error of at most 0.017.
Values may be sent and summed in bfloat16 or wider, within the bound.
No kernel may reach another device: no remote copies, remote signals or barrier semaphores. Data moves between devices by JAX's collectives and lax.ppermute only.
A program may use at most 64 MiB of HBM per device.

v0:
```python
import jax
import jax.numpy as jnp
from jax import lax
from jax.sharding import PartitionSpec as P

H = 48
KVH = 8
HD = 128


def expert_rows(segments):
    gate_pieces = [
        jnp.dot(segment[0], segment[1], preferred_element_type=jnp.float32) for segment in segments
    ]
    up_pieces = [
        jnp.dot(segment[0], segment[2], preferred_element_type=jnp.float32) for segment in segments
    ]
    gate_part = gate_pieces[0]
    up_part = up_pieces[0]
    gate_share, up_share = (
        lax.psum_scatter(
            gate_part.astype(jnp.bfloat16), "ep", scatter_dimension=1, tiled=True
        ).astype(jnp.float32),
        lax.psum_scatter(
            up_part.astype(jnp.bfloat16), "ep", scatter_dimension=1, tiled=True
        ).astype(jnp.float32),
    )
    hidden_share = (jax.nn.silu(gate_share) * up_share).astype(jnp.bfloat16)
    row_counts = [segment[0].shape[0] for segment in segments]
    piece_rows = lax.all_gather(hidden_share, "ep", axis=1, tiled=True)
    products = []
    offset = 0
    for segment, row_count in zip(segments, row_counts):
        weight_rows = segment[3]
        products.append(jnp.dot(piece_rows, weight_rows, preferred_element_type=jnp.float32))
        offset = offset + row_count
    produced = products[0]
    return produced.astype(jnp.bfloat16)


def on_device(queries, keys, values, gate_weight, up_weight, down_weight, expert_ids, route_logits):
    tok_rows = queries.shape[0]
    my_index = lax.axis_index("ctx")
    kv_local = keys.shape[1] // HD
    groups = H // KVH
    score_scale = HD ** (-0.5)
    query_heads = queries.reshape(tok_rows, kv_local, groups, HD)
    query_pos = my_index * tok_rows + jnp.arange(tok_rows, dtype=jnp.int32)
    row_top = jnp.full((kv_local, groups, tok_rows), -1e30, jnp.float32)
    key_piece = lax.all_gather(keys, "ctx", axis=0, tiled=True)
    value_piece = lax.all_gather(values, "ctx", axis=0, tiled=True)
    length = key_piece.shape[0]
    key_heads = key_piece.reshape(length, kv_local, HD)
    value_heads = value_piece.reshape(length, kv_local, HD)
    scores = (
        jnp.einsum("tkgd,nkd->kgtn", query_heads, key_heads, preferred_element_type=jnp.float32)
        * score_scale
    )
    allowed = query_pos[:, None] >= jnp.arange(length, dtype=jnp.int32)[None, :]
    scores = jnp.where(allowed, scores, -1e30)
    new_top = jnp.maximum(row_top, jnp.max(scores, axis=-1))
    weights = jnp.where(allowed, jnp.exp(scores - new_top[..., None]), 0.0)
    row_total = jnp.sum(weights, axis=-1)
    running = jnp.einsum(
        "kgtn,nkd->kgtd",
        weights.astype(jnp.bfloat16),
        value_heads,
        preferred_element_type=jnp.float32,
    )
    row_top, row_total, running = (new_top, row_total, running)
    head_out = running / row_total[..., None]
    attended = (
        head_out.transpose(2, 0, 1, 3)
        .reshape(tok_rows, kv_local * groups * HD)
        .astype(jnp.bfloat16)
    )
    experts = lax.axis_size("ctx")
    features = attended.shape[1]
    hot_cap = 6 * tok_rows // experts
    flat_ids = expert_ids.reshape(-1)
    expert_range = jnp.arange(experts, dtype=jnp.int32)
    hit_table = (flat_ids[:, None] == expert_range[None, :]).astype(jnp.int32)
    slot_of = jnp.sum((jnp.cumsum(hit_table, axis=0) - 1) * hit_table, axis=1)
    own_gate = gate_weight[0]
    own_up = up_weight[0]
    own_down = down_weight[0]
    target = flat_ids * hot_cap + slot_of
    slot_total = experts * hot_cap
    placer = (jnp.arange(slot_total, dtype=jnp.int32)[:, None] == target[None, :]).astype(
        jnp.bfloat16
    )
    placer = jnp.sum(placer.reshape(slot_total, tok_rows, 2), axis=2)
    placed = jnp.dot(placer, attended, preferred_element_type=jnp.float32).astype(jnp.bfloat16)
    outgoing = placed.reshape(experts, hot_cap, features)
    arrived = lax.all_to_all(outgoing, "ctx", split_axis=0, concat_axis=0, tiled=True)
    segments = [(arrived.reshape(experts * hot_cap, features), own_gate, own_up, own_down)]
    produced = expert_rows(segments)
    cold_answer = produced.reshape(experts, hot_cap, features)
    came_back = lax.all_to_all(cold_answer, "ctx", split_axis=0, concat_axis=0, tiled=True)
    answer_table = came_back.reshape(experts * hot_cap, features)
    picked = jnp.take(answer_table, target, axis=0).reshape(tok_rows, 2, features)
    route_share = jax.nn.softmax(route_logits, axis=-1)
    mixture = jnp.sum(picked.astype(jnp.float32) * route_share[:, :, None], axis=1)
    return (attended.astype(jnp.float32) + mixture).astype(jnp.bfloat16)


def solution(mesh):
    in_specs = (
        P("ctx", "ep"),
        P("ctx", "ep"),
        P("ctx", "ep"),
        P("ctx", "ep", None),
        P("ctx", "ep", None),
        P("ctx", None, "ep"),
        P("ctx", None),
        P("ctx", None),
    )
    out_specs = P("ctx", "ep")
    return jax.shard_map(
        on_device, mesh=mesh, in_specs=in_specs, out_specs=out_specs, check_vma=False
    )
```

profile of v0, /device:TPU:32, one launch (start us, length us, event | category | flops | bytes accessed | tf_op | source)
XLA Modules:
  0.0 491.0 jit_solution(1740220423678054590)
XLA Ops:
  7.3 1.6 copy.39
  10.1 1.1 iota_compare_fusion
  12.7 1.3 compare_and_fusion
  14.0 1.1 copy.37
  15.2 59.2 %all-gather.4.cloned.1.call-done = bf16[4096,128]{1,0:T(8,128)(2,1)} async-done(((bf16[128,128]{1,0:T(8,128)(2,1)}), bf16[4096,128]{1,0:T(8,128)(2,1)}) %all-gather.4.cloned.1.call-update) | async-done | bytes 1048592 | tf_op jit(solution)/shard_map/all_gather | solution.py:50
  74.4 3.4 fusion
  77.8 4.5 copy-done.1
  82.4 3.1 fusion.1
  85.5 53.3 %all-gather.6.cloned.1.call-done = bf16[4096,128]{0,1:T(8,128)(2,1)} async-done(((bf16[128,128]{0,1:T(8,128)(2,1)}), bf16[4096,128]{0,1:T(8,128)(2,1)}) %all-gather.6.cloned.1.call-update) | async-done | bytes 1048592 | tf_op jit(solution)/shard_map/all_gather | solution.py:51
  138.8 8.1 %fusion.22 = bf16[6,128,128]{1,2,0:T(8,128)(2,1)S(1)} fusion(f32[4096,128,6]{1,0,2:T(8,128)} %copy-done.1, f32[6,128]{1,0:T(8,128)S(1)} %broadcast_maximum_fusion, pred[128,4096]{0,1:T(8,128)(4,1)} %iota_compare_fusion, bf16[4096,128]{0,1:T(8,128)(2,1)} %all-gather.6.cloned.1.call-done, f32[6,128]{1,0:T(8,128)S(1)} %fusion.1), kind=kOutput, calls=%fused_computation.22 | convolution fusion | flops 821231616 | bytes 14358528 | tf_op jit(solution)/shard_map/kgtn,nkd->kgtd/dot_general | solution.py:64
  147.4 36.9 %all_to_all.10 = bf16[32,24,768]{2,1,0:T(8,128)(2,1)S(1)} all-to-all(bf16[32,24,768]{2,1,0:T(8,128)(2,1)S(1)} %bitcast.82), channel_id=1, replica_groups=mesh['ctx'=32,'ep'=8] {'ctx'}, dimensions={0} | all-to-all | bytes 2359296 | tf_op jit(solution)/shard_map/all_to_all | solution.py:95
  185.4 4.0 convolution_convert_fusion.1
  189.4 6.6 %convolution_convert_fusion = bf16[768,2048]{1,0:T(8,128)(2,1)} fusion(bf16[768,768]{1,0:T(8,128)(2,1)} %bitcast.85, bf16[1,768,2048]{2,1,0:T(8,128)(2,1)} %param.12), kind=kOutput, calls=%fused_computation.9 | convolution fusion | flops 2417491968 | bytes 7471104 | tf_op jit(solution)/shard_map/dot_general | solution.py:16
  196.3 75.8 %reduce-scatter.3.cloned.1.call-done = bf16[768,256]{1,0:T(8,128)(2,1)} async-done(((bf16[768,2048]{1,0:T(8,128)(2,1)}), bf16[768,256]{1,0:T(8,128)(2,1)}) %reduce-scatter.3.cloned.1.call-update) | async-done | bytes 393232 | tf_op jit(solution)/shard_map/reduce_scatter | solution.py:21
  272.0 88.2 %reduce-scatter.5.cloned.1.call-done = bf16[768,256]{1,0:T(8,128)(2,1)} async-done(((bf16[768,2048]{1,0:T(8,128)(2,1)}), bf16[768,256]{1,0:T(8,128)(2,1)}) %reduce-scatter.5.cloned.1.call-update) | async-done | bytes 393232 | tf_op jit(solution)/shard_map/reduce_scatter | solution.py:24
  360.3 2.1 fusion.31
  362.4 67.5 %all-gather.8.cloned.1.call-done = bf16[768,2048]{1,0:T(8,128)(2,1)} async-done(((bf16[768,256]{1,0:T(8,128)(2,1)}), bf16[768,2048]{1,0:T(8,128)(2,1)}) %all-gather.8.cloned.1.call-update) | async-done | bytes 3145744 | tf_op jit(solution)/shard_map/all_gather | solution.py:30
  429.9 6.5 %fusion.11 = bf16[768,768]{1,0:T(8,128)(2,1)} fusion(bf16[768,2048]{1,0:T(8,128)(2,1)} %all-gather.8.cloned.1.call-done, bf16[1,2048,768]{2,1,0:T(8,128)(2,1)} %param.13), kind=kOutput, calls=%fused_computation.16 | convolution fusion | flops 2416508928 | bytes 7471104 | tf_op jit(solution)/shard_map/dot_general | solution.py:35
  436.4 7.7 %all-to-all-start.1 = ((bf16[32,24,768]{2,1,0:T(8,128)(2,1)}), bf16[32,24,768]{2,1,0:T(8,128)(2,1)}, u32[]{:S(2)}, u32[]{:S(2)}) async-start(bf16[32,24,768]{2,1,0:T(8,128)(2,1)} %bitcast.83), calls=%async_computation.3 | async-start | bytes 2359296 | tf_op jit(solution)/shard_map/all_to_all | solution.py:99
  446.2 29.8 %all-to-all-done.1 = bf16[32,24,768]{2,1,0:T(8,128)(2,1)} async-done(((bf16[32,24,768]{2,1,0:T(8,128)(2,1)}), bf16[32,24,768]{2,1,0:T(8,128)(2,1)}, u32[]{:S(2)}, u32[]{:S(2)}) %all-to-all-start.1) | async-done | bytes 1179680 | tf_op jit(solution)/shard_map/all_to_all | solution.py:99
  475.9 3.6 gather_fusion
  479.5 1.1 gather.7
  480.7 2.1 multiply_reduce_fusion
  482.8 1.7 add_convert_fusion
  (53 shorter events, 7.3 us)
Async XLA Ops:
  6.5 178.8 %copy-start = (bf16[1,768,2048]{2,1,0:T(8,128)(2,1)S(1)}, bf16[1,768,2048]{2,1,0:T(8,128)(2,1)}, u32[]{:S(2)}) copy-start(bf16[1,768,2048]{2,1,0:T(8,128)(2,1)} %param.11) | copy-start | bytes 9437188
  6.5 67.9 %all-gather.4.cloned.1.call-start = ((), (), s32[]{:S(2)}) async-start(), calls=%async_computation.4 | async-start | bytes 1081344 | tf_op jit(solution)/shard_map/all_gather | solution.py:50
  7.3 131.5 %all-gather.6.cloned.1.call-start = ((), (), s32[]{:S(2)}) async-start(), calls=%async_computation.5 | async-start | bytes 1081344 | tf_op jit(solution)/shard_map/all_gather | solution.py:51
  9.0 263.1 %reduce-scatter.3.cloned.1.call-start = ((), (), s32[]{:S(2)}) async-start(), calls=%async_computation.6 | async-start | bytes 3538944 | tf_op jit(solution)/shard_map/reduce_scatter | solution.py:21
  12.2 0.6 copy-start.4
  74.4 7.9 %copy-start.2 = (pred[128,4096]{0,1:T(8,128)(4,1)S(1)}, pred[128,4096]{0,1:T(8,128)(4,1)}, u32[]{:S(2)}) copy-start(pred[128,4096]{0,1:T(8,128)(4,1)} %iota_compare_fusion) | copy-start | bytes 1572868
  77.8 4.6 copy-start.1
  184.3 1.0 copy-start.3
  189.4 170.9 %reduce-scatter.5.cloned.1.call-start = ((), (), s32[]{:S(2)}) async-start(), calls=%async_computation.7 | async-start | bytes 3538944 | tf_op jit(solution)/shard_map/reduce_scatter | solution.py:24
  196.0 233.9 %all-gather.8.cloned.1.call-start = ((), (), s32[]{:S(2)}) async-start(), calls=%async_computation.8 | async-start | bytes 3538944 | tf_op jit(solution)/shard_map/all_gather | solution.py:30
  362.4 81.7 %copy-start.6 = (s32[128,2]{0,1:T(2,128)S(1)}, s32[128,2]{0,1:T(2,128)}, u32[]{:S(2)}) copy-start(s32[128,2]{0,1:T(2,128)} %param.14) | copy-start | bytes 3076
  362.4 82.0 %copy-start.8 = (pred[128,2]{0,1:T(4,128)(4,1)S(1)}, pred[128,2]{0,1:T(4,128)(4,1)}, u32[]{:S(2)}) copy-start(pred[128,2]{0,1:T(4,128)(4,1)} %get-tuple-element.5) | copy-start | bytes 772
  362.4 82.1 %copy-start.7 = (f32[128,2]{0,1:T(2,128)S(1)}, f32[128,2]{0,1:T(2,128)}, u32[]{:S(2)}) copy-start(f32[128,2]{0,1:T(2,128)} %param.15) | copy-start | bytes 3076
  362.4 82.9 %copy-start.5 = (s32[256]{0:T(256)S(1)}, s32[256]{0:T(256)}, u32[]{:S(2)}) copy-start(s32[256]{0:T(256)} %copy-done.4) | copy-start | bytes 3076
  436.4 39.5 %all-to-all-start.1 = ((bf16[32,24,768]{2,1,0:T(8,128)(2,1)}), bf16[32,24,768]{2,1,0:T(8,128)(2,1)}, u32[]{:S(2)}, u32[]{:S(2)}) async-start(bf16[32,24,768]{2,1,0:T(8,128)(2,1)} %bitcast.83), calls=%async_computation.3 | async-start | bytes 2359296 | tf_op jit(solution)/shard_map/all_to_all | solution.py:99
Sparse Core Ops, SparseCore 0:
  9.2 65.2 all-gather.3
  76.2 62.5 all-gather.5
  189.5 82.4 reduce-scatter.2
  276.0 84.1 reduce-scatter.4
  362.6 67.3 all-gather.7
where the time goes:
time: 491 us
  waiting for transfers between devices  375 us (76%)
  blocking collectives  36.9 us (8%)
  matrix products  29 us (6%)
  local copies, waits for them, and re-layouts  16.9 us (3%)
  between operations  13.3 us (3%)
  other arithmetic  12.2 us (2%)
  starting transfers between devices  8.04 us (2%)
    reduce_scatter x1, waiting for transfers between devices, expert_rows(): lax.psum_scatter(up_part.astype(jnp.bfloat16), 'ep', scatter_dimension=1,...  88.2 us
    reduce_scatter x1, waiting for transfers between devices, expert_rows(): lax.psum_scatter(gate_part.astype(jnp.bfloat16), 'ep', scatter_dimension=...  75.8 us
    all_gather x1, waiting for transfers between devices, expert_rows(): piece_rows = lax.all_gather(hidden_share, 'ep', axis=1, tiled=True)  67.5 us
    all_gather x1, waiting for transfers between devices, on_device(): key_piece = lax.all_gather(keys, 'ctx', axis=0, tiled=True)  59.2 us
    all_gather x1, waiting for transfers between devices, on_device(): value_piece = lax.all_gather(values, 'ctx', axis=0, tiled=True)  53.3 us
    all_to_all x1, blocking collectives, on_device(): lax.all_to_all(outgoing, 'ctx', split_axis=0, concat_axis=0, tiled=True)  36.9 us
    all_to_all x1, waiting for transfers between devices, on_device(): lax.all_to_all(cold_answer, 'ctx', split_axis=0, concat_axis=0, tiled=True)  29.8 us
  transfers between devices with their start and end apart: 6, of which 6 were waited for; matrix products, arithmetic and copies ran while one was open for 5% of the time, Pallas kernels for 0%

commit v1 on v0

--- a/solution.py
+++ b/solution.py
@@ -47,7 +47,10 @@
     query_heads = queries.reshape(tok_rows, kv_local, groups, HD)
     query_pos = my_index * tok_rows + jnp.arange(tok_rows, dtype=jnp.int32)
     row_top = jnp.full((kv_local, groups, tok_rows), -1e30, jnp.float32)
-    key_piece = lax.all_gather(keys, "ctx", axis=0, tiled=True)
+    count = lax.axis_size("ctx")
+    pieces = jnp.stack([keys for _ in range(count)])
+    pieces = lax.all_to_all(pieces, "ctx", split_axis=0, concat_axis=0)
+    key_piece = jnp.concatenate(pieces, axis=0)
     value_piece = lax.all_gather(values, "ctx", axis=0, tiled=True)
     length = key_piece.shape[0]
     key_heads = key_piece.reshape(length, kv_local, HD)

time: 491 us -> 439 us (0.89)
  waiting for transfers between devices: 375 us -> 313 us
  starting transfers between devices: 8.04 us -> 17.7 us
    all_gather x1 -> x0, waiting for transfers between devices: 59.2 us -> none  [on_device(): key_piece = lax.all_gather(keys, 'ctx', axis=0, tiled=True)]
    all_gather x1, waiting for transfers between devices: 53.3 us -> 27.3 us  [on_device(): value_piece = lax.all_gather(values, 'ctx', axis=0, tiled=True)]
    all_to_all x0 -> x1, waiting for transfers between devices: none -> 24.7 us  [on_device(): pieces = lax.all_to_all(pieces, 'ctx', split_axis=0, concat_axis=0)]
    all_to_all x0 -> x1, starting transfers between devices: none -> 9.71 us  [on_device(): pieces = lax.all_to_all(pieces, 'ctx', split_axis=0, concat_axis=0)]
where the time goes in v1:
time: 439 us; the launch traced here: 438 us
  waiting for transfers between devices  313 us (71%)
  blocking collectives  37.2 us (8%)
  matrix products  29.1 us (7%)
  starting transfers between devices  17.7 us (4%)
  local copies, waits for them, and re-layouts  16.8 us (4%)
  between operations  13.3 us (3%)
  other arithmetic  11.6 us (3%)
    reduce_scatter x1, waiting for transfers between devices, expert_rows(): lax.psum_scatter(up_part.astype(jnp.bfloat16), 'ep', scatter_dimension=1,...  88.4 us
    reduce_scatter x1, waiting for transfers between devices, expert_rows(): lax.psum_scatter(gate_part.astype(jnp.bfloat16), 'ep', scatter_dimension=...  74.9 us
    all_gather x1, waiting for transfers between devices, expert_rows(): piece_rows = lax.all_gather(hidden_share, 'ep', axis=1, tiled=True)  67.5 us
    all_to_all x1, blocking collectives, on_device(): lax.all_to_all(outgoing, 'ctx', split_axis=0, concat_axis=0, tiled=True)  37.2 us
    all_to_all x1, waiting for transfers between devices, on_device(): lax.all_to_all(cold_answer, 'ctx', split_axis=0, concat_axis=0, tiled=True)  29.8 us
    all_gather x1, waiting for transfers between devices, on_device(): value_piece = lax.all_gather(values, 'ctx', axis=0, tiled=True)  27.3 us
    all_to_all x1, waiting for transfers between devices, on_device(): pieces = lax.all_to_all(pieces, 'ctx', split_axis=0, concat_axis=0)  24.7 us
    all_to_all x1, starting transfers between devices, on_device(): pieces = lax.all_to_all(pieces, 'ctx', split_axis=0, concat_axis=0)  9.71 us
  transfers between devices with their start and end apart: 6, of which 6 were waited for; matrix products, arithmetic and copies ran while one was open for 5% of the time, Pallas kernels for 0%

profile of v1, /device:TPU:32, one launch (start us, length us, event | category | flops | bytes accessed | tf_op | source)
XLA Modules:
  0.0 438.3 jit_solution(3789201431100860066)
XLA Ops:
  6.5 2.2 stack.2
  8.7 9.7 %all-to-all-start = ((bf16[32,128,128]{2,1,0:T(8,128)(2,1)}), bf16[32,128,128]{2,1,0:T(8,128)(2,1)}, u32[]{:S(2)}, u32[]{:S(2)}) async-start(bf16[32,128,128]{2,1,0:T(8,128)(2,1)} %stack.2), calls=%async_computation | async-start | bytes 2097152 | tf_op jit(solution)/shard_map/all_to_all | solution.py:52
  20.9 1.2 iota_compare_fusion
  23.5 24.7 %all-to-all-done = bf16[32,128,128]{2,1,0:T(8,128)(2,1)} async-done(((bf16[32,128,128]{2,1,0:T(8,128)(2,1)}), bf16[32,128,128]{2,1,0:T(8,128)(2,1)}, u32[]{:S(2)}, u32[]{:S(2)}) %all-to-all-start) | async-done | bytes 1048608 | tf_op jit(solution)/shard_map/all_to_all | solution.py:52
  48.2 3.5 fusion
  51.7 4.5 %copy-done.1 = f32[4096,128,6]{1,0,2:T(8,128)} copy-done((f32[4096,128,6]{1,0,2:T(8,128)}, f32[4096,128,6]{1,0,2:T(8,128)S(1)}, u32[]{:S(2)}) %copy-start.1) | copy-done | bytes 12582936
  56.2 3.1 fusion.1
  59.3 27.3 %all-gather.3.cloned.1.call-done = bf16[4096,128]{0,1:T(8,128)(2,1)} async-done(((bf16[128,128]{0,1:T(8,128)(2,1)}), bf16[4096,128]{0,1:T(8,128)(2,1)}) %all-gather.3.cloned.1.call-update) | async-done | bytes 1048592 | tf_op jit(solution)/shard_map/all_gather | solution.py:54
  86.6 8.1 %fusion.20 = bf16[6,128,128]{1,2,0:T(8,128)(2,1)S(1)} fusion(f32[4096,128,6]{1,0,2:T(8,128)} %copy-done.1, f32[6,128]{1,0:T(8,128)S(1)} %broadcast_maximum_fusion, pred[128,4096]{0,1:T(8,128)(4,1)} %iota_compare_fusion, bf16[4096,128]{0,1:T(8,128)(2,1)} %all-gather.3.cloned.1.call-done, f32[6,128]{1,0:T(8,128)S(1)} %fusion.1), kind=kOutput, calls=%fused_computation.20 | convolution fusion | flops 821231616 | bytes 14358528 | tf_op jit(solution)/shard_map/kgtn,nkd->kgtd/dot_general | solution.py:67
  95.2 37.2 %all_to_all.15 = bf16[32,24,768]{2,1,0:T(8,128)(2,1)S(1)} all-to-all(bf16[32,24,768]{2,1,0:T(8,128)(2,1)S(1)} %bitcast.81), channel_id=1, replica_groups=mesh['ctx'=32,'ep'=8] {'ctx'}, dimensions={0} | all-to-all | bytes 2359296 | tf_op jit(solution)/shard_map/all_to_all | solution.py:98
  132.3 1.0 copy-done.3
  133.4 4.0 convolution_convert_fusion.1
  137.5 6.6 %convolution_convert_fusion = bf16[768,2048]{1,0:T(8,128)(2,1)} fusion(bf16[768,768]{1,0:T(8,128)(2,1)} %bitcast.84, bf16[1,768,2048]{2,1,0:T(8,128)(2,1)} %param.12), kind=kOutput, calls=%fused_computation.9 | convolution fusion | flops 2417491968 | bytes 7471104 | tf_op jit(solution)/shard_map/dot_general | solution.py:16
  144.3 74.9 %reduce-scatter.3.cloned.1.call-done = bf16[768,256]{1,0:T(8,128)(2,1)} async-done(((bf16[768,2048]{1,0:T(8,128)(2,1)}), bf16[768,256]{1,0:T(8,128)(2,1)}) %reduce-scatter.3.cloned.1.call-update) | async-done | bytes 393232 | tf_op jit(solution)/shard_map/reduce_scatter | solution.py:21
  219.2 88.4 %reduce-scatter.5.cloned.1.call-done = bf16[768,256]{1,0:T(8,128)(2,1)} async-done(((bf16[768,2048]{1,0:T(8,128)(2,1)}), bf16[768,256]{1,0:T(8,128)(2,1)}) %reduce-scatter.5.cloned.1.call-update) | async-done | bytes 393232 | tf_op jit(solution)/shard_map/reduce_scatter | solution.py:24
  307.6 2.1 fusion.29
  309.8 67.5 %all-gather.5.cloned.1.call-done = bf16[768,2048]{1,0:T(8,128)(2,1)} async-done(((bf16[768,256]{1,0:T(8,128)(2,1)}), bf16[768,2048]{1,0:T(8,128)(2,1)}) %all-gather.5.cloned.1.call-update) | async-done | bytes 3145744 | tf_op jit(solution)/shard_map/all_gather | solution.py:30
  377.3 6.5 %fusion.11 = bf16[768,768]{1,0:T(8,128)(2,1)} fusion(bf16[768,2048]{1,0:T(8,128)(2,1)} %all-gather.5.cloned.1.call-done, bf16[1,2048,768]{2,1,0:T(8,128)(2,1)} %param.13), kind=kOutput, calls=%fused_computation.16 | convolution fusion | flops 2416508928 | bytes 7471104 | tf_op jit(solution)/shard_map/dot_general | solution.py:35
  383.7 7.7 %all-to-all-start.2 = ((bf16[32,24,768]{2,1,0:T(8,128)(2,1)}), bf16[32,24,768]{2,1,0:T(8,128)(2,1)}, u32[]{:S(2)}, u32[]{:S(2)}) async-start(bf16[32,24,768]{2,1,0:T(8,128)(2,1)} %bitcast.82), calls=%async_computation.4 | async-start | bytes 2359296 | tf_op jit(solution)/shard_map/all_to_all | solution.py:102
  393.5 29.8 %all-to-all-done.2 = bf16[32,24,768]{2,1,0:T(8,128)(2,1)} async-done(((bf16[32,24,768]{2,1,0:T(8,128)(2,1)}), bf16[32,24,768]{2,1,0:T(8,128)(2,1)}, u32[]{:S(2)}, u32[]{:S(2)}) %all-to-all-start.2) | async-done | bytes 1179680 | tf_op jit(solution)/shard_map/all_to_all | solution.py:102
  423.3 3.6 gather_fusion
  426.9 1.1 gather.7
  428.0 2.1 multiply_reduce_fusion
  430.1 1.7 add_convert_fusion
  (57 shorter events, 6.6 us)
Async XLA Ops:
  6.5 126.8 %copy-start = (bf16[1,768,2048]{2,1,0:T(8,128)(2,1)S(1)}, bf16[1,768,2048]{2,1,0:T(8,128)(2,1)}, u32[]{:S(2)}) copy-start(bf16[1,768,2048]{2,1,0:T(8,128)(2,1)} %param.11) | copy-start | bytes 9437188
  6.5 12.0 %copy-start.5 = (bf16[128,128]{1,0:T(8,128)(2,1)S(1)}, bf16[128,128]{1,0:T(8,128)(2,1)}, u32[]{:S(2)}) copy-start(bf16[128,128]{1,0:T(8,128)(2,1)} %param.10) | copy-start | bytes 98308
  6.5 12.7 %copy-start.8 = (s32[128,2]{0,1:T(2,128)S(1)}, s32[128,2]{0,1:T(2,128)}, u32[]{:S(2)}) copy-start(s32[128,2]{0,1:T(2,128)} %param.14) | copy-start | bytes 3076
  6.5 16.0 %copy-start.4 = (bf16[128,768]{1,0:T(8,128)(2,1)S(1)}, bf16[128,768]{1,0:T(8,128)(2,1)}, u32[]{:S(2)}) copy-start(bf16[128,768]{1,0:T(8,128)(2,1)} %param.8) | copy-start | bytes 589828
  8.7 39.4 %all-to-all-start = ((bf16[32,128,128]{2,1,0:T(8,128)(2,1)}), bf16[32,128,128]{2,1,0:T(8,128)(2,1)}, u32[]{:S(2)}, u32[]{:S(2)}) async-start(bf16[32,128,128]{2,1,0:T(8,128)(2,1)} %stack.2), calls=%async_computation | async-start | bytes 2097152 | tf_op jit(solution)/shard_map/all_to_all | solution.py:52
  18.4 68.1 %all-gather.3.cloned.1.call-start = ((), (), s32[]{:S(2)}) async-start(), calls=%async_computation.5 | async-start | bytes 1081344 | tf_op jit(solution)/shard_map/all_gather | solution.py:54
  19.2 200.0 %reduce-scatter.3.cloned.1.call-start = ((), (), s32[]{:S(2)}) async-start(), calls=%async_computation.6 | async-start | bytes 3538944 | tf_op jit(solution)/shard_map/reduce_scatter | solution.py:21
  20.6 2.8 copy-start.6
  48.2 8.0 %copy-start.2 = (pred[128,4096]{0,1:T(8,128)(4,1)S(1)}, pred[128,4096]{0,1:T(8,128)(4,1)}, u32[]{:S(2)}) copy-start(pred[128,4096]{0,1:T(8,128)(4,1)} %iota_compare_fusion) | copy-start | bytes 1572868
  51.6 4.6 %copy-start.1 = (f32[4096,128,6]{1,0,2:T(8,128)}, f32[4096,128,6]{1,0,2:T(8,128)S(1)}, u32[]{:S(2)}) copy-start(f32[4096,128,6]{1,0,2:T(8,128)S(1)} %get-tuple-element.8) | copy-start | bytes 37748740
  132.3 1.0 copy-start.3
  137.4 170.2 %reduce-scatter.5.cloned.1.call-start = ((), (), s32[]{:S(2)}) async-start(), calls=%async_computation.7 | async-start | bytes 3538944 | tf_op jit(solution)/shard_map/reduce_scatter | solution.py:24
  144.0 233.2 %all-gather.5.cloned.1.call-start = ((), (), s32[]{:S(2)}) async-start(), calls=%async_computation.8 | async-start | bytes 3538944 | tf_op jit(solution)/shard_map/all_gather | solution.py:30
  309.7 82.0 %copy-start.10 = (pred[128,2]{0,1:T(4,128)(4,1)S(1)}, pred[128,2]{0,1:T(4,128)(4,1)}, u32[]{:S(2)}) copy-start(pred[128,2]{0,1:T(4,128)(4,1)} %get-tuple-element.5) | copy-start | bytes 772
  309.7 82.1 %copy-start.9 = (f32[128,2]{0,1:T(2,128)S(1)}, f32[128,2]{0,1:T(2,128)}, u32[]{:S(2)}) copy-start(f32[128,2]{0,1:T(2,128)} %param.15) | copy-start | bytes 3076
  309.7 82.9 %copy-start.7 = (s32[256]{0:T(256)S(1)}, s32[256]{0:T(256)}, u32[]{:S(2)}) copy-start(s32[256]{0:T(256)} %copy-done.6) | copy-start | bytes 3076
  383.7 39.5 %all-to-all-start.2 = ((bf16[32,24,768]{2,1,0:T(8,128)(2,1)}), bf16[32,24,768]{2,1,0:T(8,128)(2,1)}, u32[]{:S(2)}, u32[]{:S(2)}) async-start(bf16[32,24,768]{2,1,0:T(8,128)(2,1)} %bitcast.82), calls=%async_computation.4 | async-start | bytes 2359296 | tf_op jit(solution)/shard_map/all_to_all | solution.py:102
Sparse Core Ops, SparseCore 0:
  21.0 65.5 all-gather.2
  137.5 81.6 reduce-scatter.2
  223.3 84.1 reduce-scatter.4
  309.9 67.3 all-gather.4
